TPU v7x, 128 devices: a whole 4x4x4 slice. The times are simulated.
128 devices in a mesh: region: 8 (over y, core), slab: 16 (over x, z).
Axes of the slice: x: 4, y: 4, z: 4, core: 2. Of those that a mesh axis runs over, the one named last changes fastest.
Arguments:
- coarse: float32 [32, 176, 8, 256], P('region', 'slab'), may hold values from -6 to 6
- cover: int32 [8, 16, 16, 3], replicated, may hold values from 0 to 175, as said below
- sizes: int32 [8, 2], replicated, may hold values from 6 to 16, as said below
- tclass: int32 [8, 48, 192], P('region'), may hold values from 0 to 15
- up_rows: float32 [384, 128], replicated, may hold values from -0.5 to 0.5
- up_cols: float32 [128, 1536], replicated, may hold values from -0.5 to 0.5
- lift: float32 [32, 64], replicated, may hold values from -1 to 1
- kernel_one: bfloat16 [3, 3, 64, 64], replicated, may hold values from -0.25 to 0.25
- kernel_two: bfloat16 [3, 3, 64, 64], replicated, may hold values from -0.25 to 0.25
- gain_table: float32 [16, 64], replicated, may hold values from 0.1 to 1.9
- shift_table: float32 [16, 64], replicated, may hold values from -3 to 3
Outputs:
- fine_out: bfloat16 [8, 384, 98304], P('region', 'slab')
Inputs may be any that keep to these rules, and one draw needn't show every extreme that they name: `cover`: for each region r there is an anchor (g, h) such that entry (r, i, j) names global block row g + i and block column (h + j) % 176 (longitude wraps around), as owner (g + i) // 4, row (g + i) % 4 and that column. `sizes`: column 0 lies in 6 to 16, column 1 in 6 to 16; in every draw one region has both full and another has both least.
All inputs are finite; a program needn't handle non-finite values.
Results may differ from a plain program's by a relative error of at most 0.0053.
Values may be sent and summed in bfloat16 or wider, within the bound.
A program may use at most 192 MiB of HBM per device.

v0:
```python
import jax
import jax.numpy as jnp
from jax import lax
from jax.sharding import PartitionSpec as P


def extended(cells, sides, width):
    for axis, dim in sides:
        count = lax.axis_size(axis)
        ends = count - 1
        head = lax.slice_in_dim(cells, 0, width, axis=dim)
        tail = lax.slice_in_dim(cells, cells.shape[dim] - width, cells.shape[dim], axis=dim)
        cells = jnp.concatenate(
            [
                lax.ppermute(tail, axis, [(i, (i + 1) % count) for i in range(ends)]),
                cells,
                lax.ppermute(head, axis, [((i + 1) % count, i) for i in range(ends)]),
            ],
            axis=dim,
        )
    return cells


def pair_kernel(kernel):
    channels = kernel.shape[2]
    empty_block = jnp.zeros((3, channels, channels), kernel.dtype)
    groups = []
    for offset in (-1, 0, 1):
        rows_in = []
        for side_in in (0, 1):
            cols_out = []
            for side_out in (0, 1):
                column = 2 * offset + side_in - side_out + 1
                if 0 <= column <= 2:
                    cols_out.append(kernel[:, column])
                else:
                    cols_out.append(empty_block)
            rows_in.append(jnp.concatenate(cols_out, axis=2))
        groups.append(jnp.concatenate(rows_in, axis=1))
    return jnp.concatenate(groups, axis=1)


def conv_pairs(padded, weights, out_rows):
    pair_count = padded.shape[1]
    zero_edge = jnp.zeros((padded.shape[0], 1, padded.shape[2]), padded.dtype)
    widened = jnp.concatenate([zero_edge, padded, zero_edge], axis=1)
    stacked = jnp.concatenate(
        [widened[:, 0:pair_count], widened[:, 1 : pair_count + 1], widened[:, 2 : pair_count + 2]],
        axis=2,
    )
    summed = None
    for shift_row in range(3):
        partial_value = jnp.einsum(
            "ypk,kn->ypn",
            stacked[shift_row : shift_row + out_rows],
            weights[shift_row],
            preferred_element_type=jnp.float32,
        )
        summed = partial_value if summed is None else summed + partial_value
    return summed


def local(
    coarse,
    cover,
    sizes,
    tclass,
    up_rows,
    up_cols,
    lift,
    kernel_one,
    kernel_two,
    gain_table,
    shift_table,
):
    band = lax.all_gather(coarse, "slab", axis=1, tiled=True)
    n_slab = lax.axis_size("slab")
    owner = lax.axis_index("region")
    slab_index = lax.axis_index("slab")
    block_rows = cover.shape[1]
    block_cols = cover.shape[2]
    block_height = band.shape[2]
    block_span = band.shape[3]
    in_channels = lift.shape[0]
    channels = lift.shape[1]
    fine_rows = up_rows.shape[0]
    fine_cols = up_cols.shape[1]
    rows_dev = fine_rows // n_slab
    pair_count = fine_cols // 2
    col_share = block_cols // n_slab
    rows_full = up_rows.reshape(fine_rows, block_rows, block_height)
    covered = cover
    covered = lax.dynamic_slice_in_dim(covered, slab_index * col_share, col_share, 2)
    blocks = band[covered[..., 1], covered[..., 2]]
    mine = covered[..., 0] == owner
    blocks = jnp.where(mine[..., None, None], blocks, 0.0)
    partial_cols = lax.psum_scatter(
        jnp.einsum(
            "ykb,rkjbw->ryjw",
            rows_full,
            blocks,
            precision=lax.Precision.HIGHEST,
            preferred_element_type=jnp.float32,
        ),
        "region",
        scatter_dimension=0,
        tiled=True,
    )
    partial_rows = lax.all_to_all(partial_cols, "slab", split_axis=1, concat_axis=2, tiled=True)
    partial_rows = partial_rows[0].reshape(
        rows_dev, block_cols, block_span // in_channels, in_channels
    )
    cols_op = up_cols.reshape(block_cols, block_span // in_channels, fine_cols)
    upsampled = jnp.einsum("ykwc,kwx->ycx", partial_rows, cols_op, precision=lax.Precision.HIGHEST)
    lifted = jnp.einsum("ycx,cd->yxd", upsampled, lift, precision=lax.Precision.HIGHEST)
    lifted = lifted.reshape(rows_dev, pair_count, 2 * channels)
    region_size = sizes[owner]
    valid_rows = region_size[0] * (fine_rows // block_rows)
    valid_cols = region_size[1] * (fine_cols // block_cols)
    col_index = (
        2 * jnp.arange(pair_count, dtype=jnp.int32)[:, None]
        + jnp.arange(2 * channels, dtype=jnp.int32)[None, :] // channels
    )
    col_valid = col_index < valid_cols

    def row_valid(first_row, row_count):
        global_rows = first_row + jnp.arange(row_count, dtype=jnp.int32)
        return (global_rows, (global_rows >= 0) & (global_rows < valid_rows))

    own_rows, own_valid = row_valid(slab_index * rows_dev, rows_dev)
    inside = own_valid[:, None, None] & col_valid[None]
    fine_in = jnp.where(inside, lifted, 0.0).astype(jnp.bfloat16)
    activated = jax.nn.silu(fine_in.astype(jnp.float32)).astype(jnp.bfloat16)
    tile_count = tclass.shape[1]
    tile_cols = tclass.shape[2]
    tile_rows = fine_rows // tile_count
    class_ids = jnp.arange(gain_table.shape[0], dtype=jnp.int32)
    weights_one = pair_kernel(kernel_one)
    weights_two = pair_kernel(kernel_two)
    padded = extended(activated, (("slab", 0),), 1)
    first_conv = conv_pairs(padded, weights_one, rows_dev)
    row_count = first_conv.shape[0]
    global_rows, valid = row_valid(slab_index * rows_dev, row_count)
    tile_index = jnp.clip(global_rows // tile_rows, 0, tile_count - 1)
    row_classes = tclass[0][tile_index]
    onehot = (row_classes[..., None] == class_ids[None, None, :]).astype(jnp.float32)
    gain_rows = jnp.einsum("rtk,kc->rtc", onehot, gain_table, precision=lax.Precision.HIGHEST)
    shift_rows = jnp.einsum("rtk,kc->rtc", onehot, shift_table, precision=lax.Precision.HIGHEST)
    gain_rows = jnp.concatenate([gain_rows, gain_rows], axis=-1)
    shift_rows = jnp.concatenate([shift_rows, shift_rows], axis=-1)
    shaped = first_conv.reshape(row_count, tile_cols, pair_count // tile_cols, 2 * channels)
    modulated = shaped * gain_rows[:, :, None, :] + shift_rows[:, :, None, :]
    modulated = modulated.reshape(row_count, pair_count, 2 * channels)
    retain = valid[:, None, None] & col_valid[None]
    hidden = jnp.where(retain, jax.nn.silu(modulated), 0.0).astype(jnp.bfloat16)
    padded_hidden = extended(hidden, (("slab", 0),), 1)
    second_conv = conv_pairs(padded_hidden, weights_two, rows_dev)
    result = jnp.where(inside, fine_in.astype(jnp.float32) + second_conv, 0.0).astype(jnp.bfloat16)
    return result.reshape(1, rows_dev, pair_count * 2 * channels)


def solution(mesh):
    return jax.shard_map(
        local,
        mesh=mesh,
        in_specs=(
            P("region", "slab", None, None),
            P(),
            P(),
            P("region", None, None),
            P(),
            P(),
            P(),
            P(),
            P(),
            P(),
            P(),
        ),
        out_specs=P("region", "slab", None),
        check_vma=False,
    )
```

profile of v0, /device:TPU:96, one launch (start us, length us, event | category | flops | bytes accessed | tf_op | source)
XLA Modules:
  0.0 313.4 jit_solution(15487417491095555489)
XLA Ops:
  9.9 59.4 %all-gather.2.cloned.1.call-done = f32[4,176,8,256]{3,2,1,0:T(8,128)} async-done(((f32[4,11,8,256]{3,2,1,0:T(8,128)}), f32[4,176,8,256]{3,2,1,0:T(8,128)}) %all-gather.2.cloned.1.call-update) | async-done | bytes 5767184 | tf_op jit(solution)/shard_map/all_gather | solution.py:76
  69.3 3.5 %gather_fusion = f32[128,8,256]{2,1,0:T(8,128)S(1)} fusion(f32[4,176,8,256]{3,2,1,0:T(8,128)} %all-gather.2.cloned.1.call-done, s32[128]{0:T(128)S(1)} %reshape.210), kind=kCustom, calls=%fused_computation | custom fusion | bytes 2098176 | tf_op jit(solution)/shard_map/gather | solution.py:94
  72.8 4.6 %convolution_bitcast_fusion = f32[8,384,1,256]{1,3,0,2:T(8,128)} fusion(f32[8,16,8,256]{3,2,1,0:T(8,128)S(1)} %bitcast.104, pred[8,16]{1,0:T(8,128)(4,1)S(1)} %compare_bitcast_fusion, f32[384,16,8]{0,2,1:T(8,128)S(1)} %bitcast.106), kind=kOutput, calls=%fused_computation.27 | convolution fusion | flops 1208221696 | bytes 4391040 | tf_op jit(solution)/shard_map/ykb,rkjbw->ryjw/dot_general | solution.py:98
  86.8 26.5 %reduce-scatter.2.cloned.1.call-done = f32[1,384,1,256]{1,3,0,2:T(8,128)} async-done(((f32[8,384,1,256]{1,3,0,2:T(8,128)}), f32[1,384,1,256]{1,3,0,2:T(8,128)}) %reduce-scatter.2.cloned.1.call-update) | async-done | bytes 393232 | tf_op jit(solution)/shard_map/reduce_scatter | solution.py:97
  115.2 7.1 %all-to-all-start = ((f32[1,384,1,256]{3,0,2,1:T(1,128)}), f32[1,384,1,256]{3,0,2,1:T(1,128)S(1)}, u32[]{:S(2)}, u32[]{:S(2)}) async-start(f32[1,384,1,256]{3,0,2,1:T(1,128)} %copy.41), calls=%async_computation.1 | async-start | bytes 786432 | tf_op jit(solution)/shard_map/all_to_all | solution.py:109
  125.3 3.4 %copy.47 = f32[24,192,128]{2,1,0:T(8,128)} copy(f32[24,192,128]{1,2,0:T(8,128)} %pad_maximum_fusion.5) | data formatting | bytes 4718592 | tf_op jit(solution)/shard_map/concatenate | solution.py:150
  134.9 5.7 %fusion.9 = f32[24,32,1536,1]{2,1,0,3:T(8,128)S(1)} fusion(f32[24,16,8,32]{3,2,0,1:T(8,128)} %reshape_squeeze.3, f32[128,1536]{1,0:T(8,128)S(1)} %copy-done), kind=kOutput, calls=%fused_computation.29 | convolution fusion | flops 1811939328 | bytes 5898240 | tf_op jit(solution)/shard_map/ykwc,kwx->ycx/dot_general | solution.py:114
  140.6 31.9 %fusion.7 = bf16[24,1536,64]{2,1,0:T(8,128)(2,1)} fusion(f32[24,32,1536,1]{2,1,0,3:T(8,128)S(1)} %fusion.9, f32[32,64]{1,0:T(8,128)S(1)} %copy-done.14), kind=kOutput, calls=%fused_computation.23 | convolution fusion | flops 905969664 | bytes 9445376 | tf_op jit(solution)/shard_map/ycx,cd->yxd/dot_general | solution.py:115
  172.5 12.7 %reshape.206 = bf16[24,768,128]{2,1,0:T(8,128)(2,1)} reshape(bf16[24,1536,64]{2,1,0:T(8,128)(2,1)} %fusion.7) | data formatting | bytes 9437184 | tf_op jit(solution)/shard_map/reshape | solution.py:116
  185.2 4.9 %fusion.3 = bf16[24,768,128]{2,1,0:T(8,128)(2,1)S(1)} fusion(bf16[24,768,128]{2,1,0:T(8,128)(2,1)} %reshape.206, pred[768,128]{1,0:T(8,128)(4,1)S(1)} %copy-done.11, pred[24]{0:T(512)(128)(4,1)S(1)} %copy-done.21), kind=kLoop, calls=%fused_computation.13 | loop fusion | flops 18874368 | bytes 9535512 | tf_op jit(solution)/shard_map/convert_element_type | solution.py:133
  197.7 5.5 %collective-permute-done.1 = bf16[1,768,128]{2,1,0:T(8,128)(2,1)S(1)} collective-permute-done((bf16[1,768,128]{2,1,0:T(8,128)(2,1)S(1)}, bf16[1,768,128]{2,1,0:T(8,128)(2,1)S(1)}, u32[]{:S(2)}, u32[]{:S(2)}) %collective-permute-start.1) | collective-permute-done | bytes 196640 | tf_op jit(solution)/shard_map/ppermute | solution.py:17
  203.9 4.0 %pad_slice_fusion.3 = (bf16[26,768,128]{2,1,0:T(8,128)(2,1)S(1)}, bf16[26,768,128]{2,1,0:T(8,128)(2,1)S(1)}) fusion(bf16[26,768,128]{2,1,0:T(8,128)(2,1)S(1)} %pad_maximum_fusion.2), kind=kLoop, calls=%fused_computation.20 | loop fusion | bytes 15335424 | tf_op jit(solution)/shard_map/slice | solution.py:48
  208.0 8.5 %fusion.21 = f32[24,768,128]{2,1,0:T(8,128)} fusion(bf16[3,384,128]{2,1,0:T(8,128)(2,1)S(1)} %copy-done.19, bf16[26,768,128]{2,1,0:T(8,128)(2,1)S(1)} %get-tuple-element.8, bf16[1,768,128]{2,1,0:T(8,128)(2,1)S(1)} %collective-permute-done.1, bf16[24,768,128]{2,1,0:T(8,128)(2,1)S(1)} %fusion.3, bf16[1,768,128]{2,1,0:T(8,128)(2,1)S(1)} %collective-permute-done, ...), kind=kOutput, calls=%fused_computation.48 | convolution fusion | flops 1888616448 | bytes 24870912 | tf_op jit(solution)/shard_map/ypk,kn->ypn/dot_general | solution.py:53
  216.5 7.4 %fusion.22 = f32[24,768,128]{2,1,0:T(8,128)} fusion(bf16[3,384,128]{2,1,0:T(8,128)(2,1)S(1)} %copy-done.19, bf16[26,768,128]{2,1,0:T(8,128)(2,1)S(1)} %get-tuple-element.8, bf16[1,768,128]{2,1,0:T(8,128)(2,1)S(1)} %collective-permute-done.1, bf16[24,768,128]{2,1,0:T(8,128)(2,1)S(1)} %fusion.3, bf16[1,768,128]{2,1,0:T(8,128)(2,1)S(1)} %collective-permute-done, ...), kind=kOutput, calls=%fused_computation.50 | convolution fusion | flops 1888616448 | bytes 24870912 | tf_op jit(solution)/shard_map/ypk,kn->ypn/dot_general | solution.py:53
  223.9 5.3 %mul.53 = f32[24,192,4,128]{3,2,1,0:T(4,128)} broadcast(f32[24,192,128]{2,1,0:T(8,128)S(1)} %copy.46), dimensions={0,1,3} | broadcast | bytes 11796480 | tf_op jit(solution)/shard_map/mul | solution.py:152
  229.2 7.0 %add.156 = f32[24,192,4,128]{3,2,1,0:T(4,128)} broadcast(f32[24,192,128]{2,1,0:T(8,128)} %copy.47), dimensions={0,1,3} | broadcast | bytes 11796480 | tf_op jit(solution)/shard_map/add | solution.py:152
  236.2 18.3 %fusion.5 = bf16[24,768,128]{2,1,0:T(8,128)(2,1)S(1)} fusion(f32[24,768,128]{2,1,0:T(8,128)} %bitcast.102, f32[24,768,128]{2,1,0:T(8,128)} %bitcast.101, f32[24,768,128]{2,1,0:T(8,128)} %fusion.22, f32[24,768,128]{2,1,0:T(8,128)} %fusion.21, pred[768,128]{1,0:T(8,128)(4,1)S(1)} %copy-done.11, pred[24]{0:T(512)(128)(4,1)S(1)} %copy-done.21, ...), kind=kOutput, calls=%fused_computation.15 | convolution fusion | flops 1914568704 | bytes 57999872 | tf_op jit(solution)/shard_map/ypk,kn->ypn/dot_general | solution.py:53
  256.5 3.9 %collective-permute-start.3 = (bf16[1,768,128]{2,1,0:T(8,128)(2,1)S(1)}, bf16[1,768,128]{2,1,0:T(8,128)(2,1)S(1)}, u32[]{:S(2)}, u32[]{:S(2)}) collective-permute-start(bf16[1,768,128]{2,1,0:T(8,128)(2,1)S(1)} %get-tuple-element.10), channel_id=1, source_target_pairs={{1,0},{2,1},{3,2},{4,3},{5,4},{6,5},{7,6},{8,7},{9,8},{10,9},{11,1... | collective-permute-start | bytes 589832 | tf_op jit(solution)/shard_map/ppermute | solution.py:17
  262.1 4.0 %collective-permute-done.3 = bf16[1,768,128]{2,1,0:T(8,128)(2,1)S(1)} collective-permute-done((bf16[1,768,128]{2,1,0:T(8,128)(2,1)S(1)}, bf16[1,768,128]{2,1,0:T(8,128)(2,1)S(1)}, u32[]{:S(2)}, u32[]{:S(2)}) %collective-permute-start.3) | collective-permute-done | bytes 196640 | tf_op jit(solution)/shard_map/ppermute | solution.py:17
  266.8 4.0 %pad_slice_fusion.1 = (bf16[26,768,128]{2,1,0:T(8,128)(2,1)S(1)}, bf16[26,768,128]{2,1,0:T(8,128)(2,1)S(1)}) fusion(bf16[26,768,128]{2,1,0:T(8,128)(2,1)S(1)} %pad_maximum_fusion.3), kind=kLoop, calls=%fused_computation.18 | loop fusion | bytes 15335424 | tf_op jit(solution)/shard_map/slice | solution.py:48
  270.9 8.0 %fusion.19 = f32[24,768,128]{2,1,0:T(8,128)} fusion(bf16[3,384,128]{2,1,0:T(8,128)(2,1)S(1)} %constant_dynamic-update-slice_fusion.2, bf16[26,768,128]{2,1,0:T(8,128)(2,1)S(1)} %get-tuple-element.6, bf16[1,768,128]{2,1,0:T(8,128)(2,1)S(1)} %collective-permute-done.3, bf16[24,768,128]{2,1,0:T(8,128)(2,1)S(1)} %fusion.5, ...), kind=kOutput, calls=%fused_computation.43 | convolution fusion | flops 1888616448 | bytes 24870912 | tf_op jit(solution)/shard_map/ypk,kn->ypn/dot_general | solution.py:53
  278.9 7.4 %fusion.20 = f32[24,768,128]{2,1,0:T(8,128)} fusion(bf16[3,384,128]{2,1,0:T(8,128)(2,1)S(1)} %constant_dynamic-update-slice_fusion.2, bf16[26,768,128]{2,1,0:T(8,128)(2,1)S(1)} %get-tuple-element.6, bf16[1,768,128]{2,1,0:T(8,128)(2,1)S(1)} %collective-permute-done.3, bf16[24,768,128]{2,1,0:T(8,128)(2,1)S(1)} %fusion.5, ...), kind=kOutput, calls=%fused_computation.45 | convolution fusion | flops 1888616448 | bytes 24870912 | tf_op jit(solution)/shard_map/ypk,kn->ypn/dot_general | solution.py:53
  286.3 13.8 %fusion.6 = bf16[24,768,128]{2,1,0:T(8,128)(2,1)} fusion(f32[24,768,128]{2,1,0:T(8,128)} %fusion.20, f32[24,768,128]{2,1,0:T(8,128)} %fusion.19, pred[768,128]{1,0:T(8,128)(4,1)S(1)} %copy-done.11, pred[24]{0:T(512)(128)(4,1)S(1)} %copy-done.21, bf16[3,384,128]{2,1,0:T(8,128)(2,1)S(1)} %constant_dynamic-update-slice_fusion.2, ...), kind=kOutput, calls=%fused_computation.16 | convolution fusion | flops 1907490816 | bytes 43844096 | tf_op jit(solution)/shard_map/ypk,kn->ypn/dot_general | solution.py:53
  300.1 6.4 %reshape.207 = bf16[1,24,98304]{2,1,0:T(8,128)(2,1)} reshape(bf16[24,768,128]{2,1,0:T(8,128)(2,1)} %fusion.6) | data formatting | bytes 9437184 | tf_op jit(solution)/shard_map/reshape | solution.py:159
  (104 shorter events, 34.9 us)
Async XLA Ops:
  6.5 128.3 %copy-start = (f32[128,1536]{1,0:T(8,128)S(1)}, f32[128,1536]{1,0:T(8,128)}, u32[]{:S(2)}) copy-start(f32[128,1536]{1,0:T(8,128)} %param.16) | copy-start | bytes 2359300
  6.5 70.9 %copy-start.20 = (s32[8,2]{0,1:T(2,128)S(1)}, s32[8,2]{0,1:T(2,128)}, u32[]{:S(2)}) copy-start(s32[8,2]{0,1:T(2,128)} %param.13) | copy-start | bytes 196
  6.5 72.3 %copy-start.7 = (s32[1,48,192]{2,1,0:T(8,128)S(1)}, s32[1,48,192]{2,1,0:T(8,128)}, u32[]{:S(2)}) copy-start(s32[1,48,192]{2,1,0:T(8,128)} %param.14) | copy-start | bytes 110596
  6.5 73.5 %copy-start.12 = (bf16[3,3,64,64]{3,2,1,0:T(8,128)(2,1)S(1)}, bf16[3,3,64,64]{3,2,1,0:T(8,128)(2,1)}, u32[]{:S(2)}) copy-start(bf16[3,3,64,64]{3,2,1,0:T(8,128)(2,1)} %param.18) | copy-start | bytes 221188
  6.5 73.9 %copy-start.15 = (f32[16,64]{1,0:T(8,128)S(1)}, f32[16,64]{1,0:T(8,128)}, u32[]{:S(2)}) copy-start(f32[16,64]{1,0:T(8,128)} %param.20) | copy-start | bytes 12292
  6.5 62.8 %all-gather.2.cloned.1.call-start = ((), (), s32[]{:S(2)}) async-start(), calls=%async_computation.2 | async-start | bytes 6127616 | tf_op jit(solution)/shard_map/all_gather | solution.py:76
  7.3 106.1 %reduce-scatter.2.cloned.1.call-start = ((), (), s32[]{:S(2)}) async-start(), calls=%async_computation.3 | async-start | bytes 3538944 | tf_op jit(solution)/shard_map/reduce_scatter | solution.py:97
  72.8 10.5 %copy-start.16 = (f32[16,64]{1,0:T(8,128)S(1)}, f32[16,64]{1,0:T(8,128)}, u32[]{:S(2)}) copy-start(f32[16,64]{1,0:T(8,128)} %param.21) | copy-start | bytes 12292
  80.4 42.0 %copy-start.18 = (bf16[3,384,128]{2,1,0:T(8,128)(2,1)}, bf16[3,384,128]{2,1,0:T(8,128)(2,1)S(1)}, u32[]{:S(2)}) copy-start(bf16[3,384,128]{2,1,0:T(8,128)(2,1)S(1)} %constant_dynamic-update-slice_fusion) | copy-start | bytes 884740
  115.2 16.4 %all-to-all-start = ((f32[1,384,1,256]{3,0,2,1:T(1,128)}), f32[1,384,1,256]{3,0,2,1:T(1,128)S(1)}, u32[]{:S(2)}, u32[]{:S(2)}) async-start(f32[1,384,1,256]{3,0,2,1:T(1,128)} %copy.41), calls=%async_computation.1 | async-start | bytes 786432 | tf_op jit(solution)/shard_map/all_to_all | solution.py:109
  131.6 9.0 %copy-start.14 = (f32[32,64]{1,0:T(8,128)S(1)}, f32[32,64]{1,0:T(8,128)}, u32[]{:S(2)}) copy-start(f32[32,64]{1,0:T(8,128)} %param.17) | copy-start | bytes 24580
  172.5 12.7 %copy-start.11 = (pred[768,128]{1,0:T(8,128)(4,1)S(1)}, pred[768,128]{1,0:T(8,128)(4,1)}, u32[]{:S(2)}) copy-start(pred[768,128]{1,0:T(8,128)(4,1)} %add_compare_fusion) | copy-start | bytes 294916
  172.5 12.7 %copy-start.21 = (pred[24]{0:T(512)(128)(4,1)S(1)}, pred[24]{0:T(512)(128)(4,1)}, u32[]{:S(2)}) copy-start(pred[24]{0:T(512)(128)(4,1)} %compare_and_fusion) | copy-start | bytes 76
  172.5 23.5 %copy-start.9 = (bf16[3,64,64]{2,1,0:T(8,128)(2,1)S(1)}, bf16[3,64,64]{2,1,0:T(8,128)(2,1)}, u32[]{:S(2)}) copy-start(bf16[3,64,64]{2,1,0:T(8,128)(2,1)} %get-tuple-element.21) | copy-start | bytes 73732
  172.5 23.6 %copy-start.10 = (bf16[3,64,64]{2,1,0:T(8,128)(2,1)S(1)}, bf16[3,64,64]{2,1,0:T(8,128)(2,1)}, u32[]{:S(2)}) copy-start(bf16[3,64,64]{2,1,0:T(8,128)(2,1)} %get-tuple-element.20) | copy-start | bytes 73732
  172.5 24.3 %copy-start.8 = (bf16[3,64,64]{2,1,0:T(8,128)(2,1)S(1)}, bf16[3,64,64]{2,1,0:T(8,128)(2,1)}, u32[]{:S(2)}) copy-start(bf16[3,64,64]{2,1,0:T(8,128)(2,1)} %get-tuple-element.19) | copy-start | bytes 73732
  190.1 26.4 %copy-start.2 = (bf16[24,768,128]{2,1,0:T(8,128)(2,1)}, bf16[24,768,128]{2,1,0:T(8,128)(2,1)S(1)}, u32[]{:S(2)}) copy-start(bf16[24,768,128]{2,1,0:T(8,128)(2,1)S(1)} %fusion.3) | copy-start | bytes 14155780
  190.2 7.6 %collective-permute-start = (bf16[1,768,128]{2,1,0:T(8,128)(2,1)S(1)}, bf16[1,768,128]{2,1,0:T(8,128)(2,1)S(1)}, u32[]{:S(2)}, u32[]{:S(2)}) collective-permute-start(bf16[1,768,128]{2,1,0:T(8,128)(2,1)S(1)} %get-tuple-element.11), channel_id=1, source_target_pairs={{0,1},{1,2},{2,3},{3,4},{4,5},{5,6},{6,7},{7,8},{8,9},{9,10},{10,1... | collective-permute-start | bytes 589832 | tf_op jit(solution)/shard_map/ppermute | solution.py:15
  193.6 9.7 %collective-permute-start.1 = (bf16[1,768,128]{2,1,0:T(8,128)(2,1)S(1)}, bf16[1,768,128]{2,1,0:T(8,128)(2,1)S(1)}, u32[]{:S(2)}, u32[]{:S(2)}) collective-permute-start(bf16[1,768,128]{2,1,0:T(8,128)(2,1)S(1)} %get-tuple-element.12), channel_id=1, source_target_pairs={{1,0},{2,1},{3,2},{4,3},{5,4},{6,5},{7,6},{8,7},{9,8},{10,9},{11,1... | collective-permute-start | bytes 589832 | tf_op jit(solution)/shard_map/ppermute | solution.py:17
  236.2 24.2 %copy-start.17 = (bf16[3,384,128]{2,1,0:T(8,128)(2,1)S(1)}, bf16[3,384,128]{2,1,0:T(8,128)(2,1)}, u32[]{:S(2)}) copy-start(bf16[3,384,128]{2,1,0:T(8,128)(2,1)} %maximum_dynamic-update-slice_fusion.2) | copy-start | bytes 884740
  254.5 7.6 %collective-permute-start.2 = (bf16[1,768,128]{2,1,0:T(8,128)(2,1)S(1)}, bf16[1,768,128]{2,1,0:T(8,128)(2,1)S(1)}, u32[]{:S(2)}, u32[]{:S(2)}) collective-permute-start(bf16[1,768,128]{2,1,0:T(8,128)(2,1)S(1)} %get-tuple-element.9), channel_id=1, source_target_pairs={{0,1},{1,2},{2,3},{3,4},{4,5},{5,6},{6,7},{7,8},{8,9},{9,10},{10,1... | collective-permute-start | bytes 589832 | tf_op jit(solution)/shard_map/ppermute | solution.py:15
  256.5 9.7 %collective-permute-start.3 = (bf16[1,768,128]{2,1,0:T(8,128)(2,1)S(1)}, bf16[1,768,128]{2,1,0:T(8,128)(2,1)S(1)}, u32[]{:S(2)}, u32[]{:S(2)}) collective-permute-start(bf16[1,768,128]{2,1,0:T(8,128)(2,1)S(1)} %get-tuple-element.10), channel_id=1, source_target_pairs={{1,0},{2,1},{3,2},{4,3},{5,4},{6,5},{7,6},{8,7},{9,8},{10,9},{11,1... | collective-permute-start | bytes 589832 | tf_op jit(solution)/shard_map/ppermute | solution.py:17
  270.9 15.4 %slice-start = ((s8[4718592]{0:T(1024)(128)(4,1)}), s8[4194304]{0:T(1024)(128)(4,1)S(1)}, s32[]{:S(2)}) async-start(s8[4718592]{0:T(1024)(128)(4,1)} %bitcast.99), calls=%async_computation.4 | async-start | bytes 8388608
  286.3 20.3 %copy-start.1 = (f32[128,1536]{1,0:T(8,128)S(1)}, f32[128,1536]{1,0:T(8,128)}, u32[]{:S(2)}) copy-start(f32[128,1536]{1,0:T(8,128)} %param.16) | copy-start | bytes 2359300
  (7 other events, 53.4 us)
Sparse Core Ops, SparseCore 0:
  9.5 59.7 all-gather.1
  77.5 35.7 reduce-scatter.1
where the time goes:
time: 314 us; the launch traced here: 313 us
  matrix products  107 us (34%)
  waiting for transfers between devices  98 us (31%)
  local copies, waits for them, and re-layouts  60.8 us (19%)
  starting transfers between devices  18.9 us (6%)
  between operations  15.2 us (5%)
  other arithmetic  13.4 us (4%)
    dot_general x6, matrix products, conv_pairs(): jnp.einsum('ypk,kn->ypn', stacked[shift_row:shift_row + out_rows], weight...  63.4 us
    all_gather x1, waiting for transfers between devices, local(): band = lax.all_gather(coarse, 'slab', axis=1, tiled=True)  59.4 us
    dot_general x1, matrix products, local(): jnp.einsum('ycx,cd->yxd', upsampled, lift, precision=lax.Precision.HIGHEST)  31.9 us
    reduce_scatter x1, waiting for transfers between devices, local(): lax.psum_scatter(jnp.einsum('ykb,rkjbw->ryjw', rows_full, blocks, precisi...  26.5 us
    reshape x1, local copies, waits for them, and re-layouts, local(): lifted = lifted.reshape(rows_dev, pair_count, 2 * channels)  12.7 us
    ppermute x2, waiting for transfers between devices, extended(): lax.ppermute(head, axis, [((i + 1) % count, i) for i in range(ends)])  9.52 us
    slice x2, local copies, waits for them, and re-layouts, conv_pairs(): widened[:, 0:pair_count]  8.07 us
    all_to_all x1, starting transfers between devices, local(): lax.all_to_all(partial_cols, 'slab', split_axis=1, concat_axis=2, tiled=T...  7.14 us
  transfers between devices with their start and end apart: 7, of which 6 were waited for; matrix products, arithmetic and copies ran while one was open for 7% of the time, Pallas kernels for 0%

commit v1 on v0

--- a/solution.py
+++ b/solution.py
@@ -73,7 +73,9 @@
     gain_table,
     shift_table,
 ):
-    band = lax.all_gather(coarse, "slab", axis=1, tiled=True)
+    band = jnp.concatenate(
+        lax.all_to_all(jnp.stack([coarse] * lax.axis_size("slab")), "slab", 0, 0), axis=1
+    )
     n_slab = lax.axis_size("slab")
     owner = lax.axis_index("region")
     slab_index = lax.axis_index("slab")

time: 314 us -> 372 us (1.18); the launches traced: 313 us -> 366 us
  waiting for transfers between devices: 98 us -> 134 us
  local copies, waits for them, and re-layouts: 60.8 us -> 68.8 us
  starting transfers between devices: 18.9 us -> 26.2 us
    all_to_all x0 -> x1, waiting for transfers between devices: none -> 79.3 us  [local(): lax.all_to_all(jnp.stack([coarse] * lax.axis_size('slab')), 'slab', 0, 0)]
    all_gather x1 -> x0, waiting for transfers between devices: 59.4 us -> none  [local(): band = lax.all_gather(coarse, 'slab', axis=1, tiled=True)]
    reduce_scatter x1, waiting for transfers between devices: 26.5 us -> 43.6 us  [local(): lax.psum_scatter(jnp.einsum('ykb,rkjbw->ryjw', rows_full, blocks, precisi...]
    all_to_all x0 -> x1, starting transfers between devices: none -> 6.99 us  [local(): lax.all_to_all(jnp.stack([coarse] * lax.axis_size('slab')), 'slab', 0, 0)]
    all_to_all x0 -> x1, local copies, waits for them, and re-layouts: none -> 5.65 us  [local(): lax.all_to_all(jnp.stack([coarse] * lax.axis_size('slab')), 'slab', 0, 0)]
    another operation x0 -> x1, local copies, waits for them, and re-layouts: none -> 4.15 us  [local(): jnp.stack([coarse] * lax.axis_size('slab'))]
  transfers between devices with their start and end apart: 7 -> 7, of which waited for: 6 -> 6; matrix products, arithmetic and copies ran while one was open for 7% -> 5% of each run, Pallas kernels for 0% -> 0%
where the time goes in v1:
time: 372 us; the launch traced here: 366 us
  waiting for transfers between devices  134 us (36%)
  matrix products  108 us (29%)
  local copies, waits for them, and re-layouts  68.8 us (18%)
  starting transfers between devices  26.2 us (7%)
  between operations  15.4 us (4%)
  other arithmetic  13.7 us (4%)
    all_to_all x1, waiting for transfers between devices, local(): lax.all_to_all(jnp.stack([coarse] * lax.axis_size('slab')), 'slab', 0, 0)  79.3 us
    dot_general x6, matrix products, conv_pairs(): jnp.einsum('ypk,kn->ypn', stacked[shift_row:shift_row + out_rows], weight...  63.6 us
    reduce_scatter x1, waiting for transfers between devices, local(): lax.psum_scatter(jnp.einsum('ykb,rkjbw->ryjw', rows_full, blocks, precisi...  43.6 us
    dot_general x1, matrix products, local(): jnp.einsum('ycx,cd->yxd', upsampled, lift, precision=lax.Precision.HIGHEST)  32.2 us
    reshape x1, local copies, waits for them, and re-layouts, local(): lifted = lifted.reshape(rows_dev, pair_count, 2 * channels)  12.7 us
    ppermute x2, waiting for transfers between devices, extended(): lax.ppermute(head, axis, [((i + 1) % count, i) for i in range(ends)])  9.53 us
    slice x2, local copies, waits for them, and re-layouts, conv_pairs(): widened[:, 0:pair_count]  8.07 us
    all_to_all x1, starting transfers between devices, local(): lax.all_to_all(partial_cols, 'slab', split_axis=1, concat_axis=2, tiled=T...  7.5 us
  transfers between devices with their start and end apart: 7, of which 6 were waited for; matrix products, arithmetic and copies ran while one was open for 5% of the time, Pallas kernels for 0%

profile of v1, /device:TPU:96, one launch (start us, length us, event | category | flops | bytes accessed | tf_op | source)
XLA Modules:
  0.0 366.1 jit_solution(14886868510685612593)
XLA Ops:
  6.5 4.2 %stack.2 = f32[16,4,11,8,256]{4,3,2,1,0:T(8,128)} broadcast(f32[4,11,8,256]{3,2,1,0:T(8,128)} %param.11), dimensions={1,2,3,4} | broadcast | bytes 6127616 | tf_op jit(solution)/shard_map/stack | solution.py:77
  10.7 7.0 %all-to-all-start = ((f32[16,4,11,8,256]{4,3,2,1,0:T(8,128)}), f32[16,4,11,8,256]{4,3,2,1,0:T(8,128)}, u32[]{:S(2)}, u32[]{:S(2)}) async-start(f32[16,4,11,8,256]{4,3,2,1,0:T(8,128)} %stack.2), calls=%async_computation | async-start | bytes 11534336 | tf_op jit(solution)/shard_map/all_to_all | solution.py:77
  18.5 79.3 %all-to-all-done = f32[16,4,11,8,256]{4,3,2,1,0:T(8,128)} async-done(((f32[16,4,11,8,256]{4,3,2,1,0:T(8,128)}), f32[16,4,11,8,256]{4,3,2,1,0:T(8,128)}, u32[]{:S(2)}, u32[]{:S(2)}) %all-to-all-start) | async-done | bytes 5767200 | tf_op jit(solution)/shard_map/all_to_all | solution.py:77
  97.8 5.7 %copy.37 = f32[16,4,11,8,256]{4,3,2,0,1:T(8,128)} copy(f32[16,4,11,8,256]{4,3,2,1,0:T(8,128)} %all-to-all-done) | data formatting | bytes 11534336 | tf_op jit(solution)/shard_map/all_to_all | solution.py:77
  107.0 4.5 %convolution_bitcast_fusion = f32[8,384,1,256]{1,3,0,2:T(8,128)} fusion(f32[8,16,8,256]{3,2,1,0:T(8,128)S(1)} %bitcast.109, pred[8,16]{1,0:T(8,128)(4,1)S(1)} %compare_bitcast_fusion, f32[384,128]{0,1:T(8,128)S(1)} %copy.38), kind=kOutput, calls=%fused_computation.27 | convolution fusion | flops 1208221696 | bytes 4391040 | tf_op jit(solution)/shard_map/ykb,rkjbw->ryjw/dot_general | solution.py:100
  120.9 43.6 %reduce-scatter.2.cloned.1.call-done = f32[1,384,1,256]{1,3,0,2:T(8,128)} async-done(((f32[8,384,1,256]{1,3,0,2:T(8,128)}), f32[1,384,1,256]{1,3,0,2:T(8,128)}) %reduce-scatter.2.cloned.1.call-update) | async-done | bytes 393232 | tf_op jit(solution)/shard_map/reduce_scatter | solution.py:99
  166.4 7.5 %all-to-all-start.1 = ((f32[1,384,1,256]{3,0,2,1:T(1,128)}), f32[1,384,1,256]{3,0,2,1:T(1,128)S(1)}, u32[]{:S(2)}, u32[]{:S(2)}) async-start(f32[1,384,1,256]{3,0,2,1:T(1,128)} %copy.39), calls=%async_computation.2 | async-start | bytes 786432 | tf_op jit(solution)/shard_map/all_to_all | solution.py:111
  186.4 5.7 %fusion.10 = f32[24,32,1536,1]{2,1,0,3:T(8,128)S(1)} fusion(f32[24,16,8,32]{3,2,0,1:T(8,128)} %reshape_squeeze.3, f32[128,1536]{1,0:T(8,128)S(1)} %copy-done), kind=kOutput, calls=%fused_computation.29 | convolution fusion | flops 1811939328 | bytes 5898240 | tf_op jit(solution)/shard_map/ykwc,kwx->ycx/dot_general | solution.py:116
  192.1 32.2 %fusion.7 = bf16[24,1536,64]{2,1,0:T(8,128)(2,1)} fusion(f32[24,32,1536,1]{2,1,0,3:T(8,128)S(1)} %fusion.10, f32[32,64]{1,0:T(8,128)S(1)} %copy-done.16), kind=kOutput, calls=%fused_computation.23 | convolution fusion | flops 905969664 | bytes 9445376 | tf_op jit(solution)/shard_map/ycx,cd->yxd/dot_general | solution.py:117
  224.3 12.7 %reshape.216 = bf16[24,768,128]{2,1,0:T(8,128)(2,1)} reshape(bf16[24,1536,64]{2,1,0:T(8,128)(2,1)} %fusion.7) | data formatting | bytes 9437184 | tf_op jit(solution)/shard_map/reshape | solution.py:118
  237.1 4.9 %fusion.3 = bf16[24,768,128]{2,1,0:T(8,128)(2,1)S(1)} fusion(bf16[24,768,128]{2,1,0:T(8,128)(2,1)} %reshape.216, pred[768,128]{1,0:T(8,128)(4,1)S(1)} %copy-done.11, pred[24]{0:T(512)(128)(4,1)S(1)} %copy-done.23), kind=kLoop, calls=%fused_computation.13 | loop fusion | flops 18874368 | bytes 9535512 | tf_op jit(solution)/shard_map/convert_element_type | solution.py:135
  249.6 5.5 %collective-permute-done.1 = bf16[1,768,128]{2,1,0:T(8,128)(2,1)S(1)} collective-permute-done((bf16[1,768,128]{2,1,0:T(8,128)(2,1)S(1)}, bf16[1,768,128]{2,1,0:T(8,128)(2,1)S(1)}, u32[]{:S(2)}, u32[]{:S(2)}) %collective-permute-start.1) | collective-permute-done | bytes 196640 | tf_op jit(solution)/shard_map/ppermute | solution.py:17
  255.9 4.0 %pad_slice_fusion.3 = (bf16[26,768,128]{2,1,0:T(8,128)(2,1)S(1)}, bf16[26,768,128]{2,1,0:T(8,128)(2,1)S(1)}) fusion(bf16[26,768,128]{2,1,0:T(8,128)(2,1)S(1)} %pad_maximum_fusion.2), kind=kLoop, calls=%fused_computation.20 | loop fusion | bytes 15335424 | tf_op jit(solution)/shard_map/slice | solution.py:48
  260.0 8.6 %fusion.21 = f32[24,768,128]{2,1,0:T(8,128)} fusion(bf16[3,384,128]{2,1,0:T(8,128)(2,1)S(1)} %copy-done.21, bf16[26,768,128]{2,1,0:T(8,128)(2,1)S(1)} %get-tuple-element.8, bf16[1,768,128]{2,1,0:T(8,128)(2,1)S(1)} %collective-permute-done.1, bf16[24,768,128]{2,1,0:T(8,128)(2,1)S(1)} %fusion.3, bf16[1,768,128]{2,1,0:T(8,128)(2,1)S(1)} %collective-permute-done, ...), kind=kOutput, calls=%fused_computation.47 | convolution fusion | flops 1888616448 | bytes 24870912 | tf_op jit(solution)/shard_map/ypk,kn->ypn/dot_general | solution.py:53
  268.7 7.3 %fusion.22 = f32[24,768,128]{2,1,0:T(8,128)} fusion(bf16[3,384,128]{2,1,0:T(8,128)(2,1)S(1)} %copy-done.21, bf16[26,768,128]{2,1,0:T(8,128)(2,1)S(1)} %get-tuple-element.8, bf16[1,768,128]{2,1,0:T(8,128)(2,1)S(1)} %collective-permute-done.1, bf16[24,768,128]{2,1,0:T(8,128)(2,1)S(1)} %fusion.3, bf16[1,768,128]{2,1,0:T(8,128)(2,1)S(1)} %collective-permute-done, ...), kind=kOutput, calls=%fused_computation.49 | convolution fusion | flops 1888616448 | bytes 24870912 | tf_op jit(solution)/shard_map/ypk,kn->ypn/dot_general | solution.py:53
  276.0 5.3 %mul.53 = f32[24,192,4,128]{3,2,1,0:T(4,128)} broadcast(f32[24,192,128]{2,1,0:T(8,128)S(1)} %copy.44), dimensions={0,1,3} | broadcast | bytes 11796480 | tf_op jit(solution)/shard_map/mul | solution.py:154
  281.3 7.0 %add.156 = f32[24,192,4,128]{3,2,1,0:T(4,128)} broadcast(f32[24,192,128]{2,1,0:T(8,128)} %copy.45), dimensions={0,1,3} | broadcast | bytes 11796480 | tf_op jit(solution)/shard_map/add | solution.py:154
  288.3 18.3 %fusion.5 = bf16[24,768,128]{2,1,0:T(8,128)(2,1)S(1)} fusion(f32[24,768,128]{2,1,0:T(8,128)} %bitcast.106, f32[24,768,128]{2,1,0:T(8,128)} %bitcast.105, f32[24,768,128]{2,1,0:T(8,128)} %fusion.22, f32[24,768,128]{2,1,0:T(8,128)} %fusion.21, pred[768,128]{1,0:T(8,128)(4,1)S(1)} %copy-done.11, pred[24]{0:T(512)(128)(4,1)S(1)} %copy-done.23, ...), kind=kOutput, calls=%fused_computation.15 | convolution fusion | flops 1914568704 | bytes 57999872 | tf_op jit(solution)/shard_map/ypk,kn->ypn/dot_general | solution.py:53
  314.2 4.0 %collective-permute-done.3 = bf16[1,768,128]{2,1,0:T(8,128)(2,1)S(1)} collective-permute-done((bf16[1,768,128]{2,1,0:T(8,128)(2,1)S(1)}, bf16[1,768,128]{2,1,0:T(8,128)(2,1)S(1)}, u32[]{:S(2)}, u32[]{:S(2)}) %collective-permute-start.3) | collective-permute-done | bytes 196640 | tf_op jit(solution)/shard_map/ppermute | solution.py:17
  319.2 4.0 %pad_slice_fusion.1 = (bf16[26,768,128]{2,1,0:T(8,128)(2,1)S(1)}, bf16[26,768,128]{2,1,0:T(8,128)(2,1)S(1)}) fusion(bf16[26,768,128]{2,1,0:T(8,128)(2,1)S(1)} %pad_maximum_fusion.3), kind=kLoop, calls=%fused_computation.18 | loop fusion | bytes 15335424 | tf_op jit(solution)/shard_map/slice | solution.py:48
  323.2 8.1 %fusion.19 = f32[24,768,128]{2,1,0:T(8,128)} fusion(bf16[3,384,128]{2,1,0:T(8,128)(2,1)S(1)} %constant_dynamic-update-slice_fusion.2, bf16[26,768,128]{2,1,0:T(8,128)(2,1)S(1)} %get-tuple-element.6, bf16[1,768,128]{2,1,0:T(8,128)(2,1)S(1)} %collective-permute-done.3, bf16[24,768,128]{2,1,0:T(8,128)(2,1)S(1)} %fusion.5, ...), kind=kOutput, calls=%fused_computation.42 | convolution fusion | flops 1888616448 | bytes 24870912 | tf_op jit(solution)/shard_map/ypk,kn->ypn/dot_general | solution.py:53
  331.3 7.4 %fusion.20 = f32[24,768,128]{2,1,0:T(8,128)} fusion(bf16[3,384,128]{2,1,0:T(8,128)(2,1)S(1)} %constant_dynamic-update-slice_fusion.2, bf16[26,768,128]{2,1,0:T(8,128)(2,1)S(1)} %get-tuple-element.6, bf16[1,768,128]{2,1,0:T(8,128)(2,1)S(1)} %collective-permute-done.3, bf16[24,768,128]{2,1,0:T(8,128)(2,1)S(1)} %fusion.5, ...), kind=kOutput, calls=%fused_computation.44 | convolution fusion | flops 1888616448 | bytes 24870912 | tf_op jit(solution)/shard_map/ypk,kn->ypn/dot_general | solution.py:53
  338.7 13.8 %fusion.6 = bf16[24,768,128]{2,1,0:T(8,128)(2,1)} fusion(f32[24,768,128]{2,1,0:T(8,128)} %fusion.20, f32[24,768,128]{2,1,0:T(8,128)} %fusion.19, pred[768,128]{1,0:T(8,128)(4,1)S(1)} %copy-done.11, pred[24]{0:T(512)(128)(4,1)S(1)} %copy-done.23, bf16[3,384,128]{2,1,0:T(8,128)(2,1)S(1)} %constant_dynamic-update-slice_fusion.2, ...), kind=kOutput, calls=%fused_computation.16 | convolution fusion | flops 1907490816 | bytes 43844096 | tf_op jit(solution)/shard_map/ypk,kn->ypn/dot_general | solution.py:53
  352.6 6.4 %reshape.217 = bf16[1,24,98304]{2,1,0:T(8,128)(2,1)} reshape(bf16[24,768,128]{2,1,0:T(8,128)(2,1)} %fusion.6) | data formatting | bytes 9437184 | tf_op jit(solution)/shard_map/reshape | solution.py:161
  (109 shorter events, 43.5 us)
Async XLA Ops:
  6.5 179.8 %copy-start = (f32[128,1536]{1,0:T(8,128)S(1)}, f32[128,1536]{1,0:T(8,128)}, u32[]{:S(2)}) copy-start(f32[128,1536]{1,0:T(8,128)} %param.16) | copy-start | bytes 2359300
  6.5 11.2 %copy-start.12 = (s32[8,16,16,3]{2,1,3,0:T(8,128)S(1)}, s32[8,16,16,3]{2,1,3,0:T(8,128)}, u32[]{:S(2)}) copy-start(s32[8,16,16,3]{2,1,3,0:T(8,128)} %param.12) | copy-start | bytes 73732
  6.5 11.8 %copy-start.13 = (f32[384,128]{1,0:T(8,128)S(1)}, f32[384,128]{1,0:T(8,128)}, u32[]{:S(2)}) copy-start(f32[384,128]{1,0:T(8,128)} %param.15) | copy-start | bytes 589828
  10.7 87.1 %all-to-all-start = ((f32[16,4,11,8,256]{4,3,2,1,0:T(8,128)}), f32[16,4,11,8,256]{4,3,2,1,0:T(8,128)}, u32[]{:S(2)}, u32[]{:S(2)}) async-start(f32[16,4,11,8,256]{4,3,2,1,0:T(8,128)} %stack.2), calls=%async_computation | async-start | bytes 11534336 | tf_op jit(solution)/shard_map/all_to_all | solution.py:77
  17.7 146.8 %reduce-scatter.2.cloned.1.call-start = ((), (), s32[]{:S(2)}) async-start(), calls=%async_computation.3 | async-start | bytes 3538944 | tf_op jit(solution)/shard_map/reduce_scatter | solution.py:99
  111.5 8.8 %copy-start.15 = (bf16[3,3,64,64]{3,2,1,0:T(8,128)(2,1)S(1)}, bf16[3,3,64,64]{3,2,1,0:T(8,128)(2,1)}, u32[]{:S(2)}) copy-start(bf16[3,3,64,64]{3,2,1,0:T(8,128)(2,1)} %param.19) | copy-start | bytes 221188
  114.5 59.4 %copy-start.20 = (bf16[3,384,128]{2,1,0:T(8,128)(2,1)}, bf16[3,384,128]{2,1,0:T(8,128)(2,1)S(1)}, u32[]{:S(2)}) copy-start(bf16[3,384,128]{2,1,0:T(8,128)(2,1)S(1)} %constant_dynamic-update-slice_fusion) | copy-start | bytes 884740
  166.4 16.7 %all-to-all-start.1 = ((f32[1,384,1,256]{3,0,2,1:T(1,128)}), f32[1,384,1,256]{3,0,2,1:T(1,128)S(1)}, u32[]{:S(2)}, u32[]{:S(2)}) async-start(f32[1,384,1,256]{3,0,2,1:T(1,128)} %copy.39), calls=%async_computation.2 | async-start | bytes 786432 | tf_op jit(solution)/shard_map/all_to_all | solution.py:111
  183.1 9.0 %copy-start.16 = (f32[32,64]{1,0:T(8,128)S(1)}, f32[32,64]{1,0:T(8,128)}, u32[]{:S(2)}) copy-start(f32[32,64]{1,0:T(8,128)} %param.17) | copy-start | bytes 24580
  224.3 12.7 %copy-start.11 = (pred[768,128]{1,0:T(8,128)(4,1)S(1)}, pred[768,128]{1,0:T(8,128)(4,1)}, u32[]{:S(2)}) copy-start(pred[768,128]{1,0:T(8,128)(4,1)} %add_compare_fusion) | copy-start | bytes 294916
  224.3 12.7 %copy-start.23 = (pred[24]{0:T(512)(128)(4,1)S(1)}, pred[24]{0:T(512)(128)(4,1)}, u32[]{:S(2)}) copy-start(pred[24]{0:T(512)(128)(4,1)} %compare_and_fusion) | copy-start | bytes 76
  224.3 23.5 %copy-start.9 = (bf16[3,64,64]{2,1,0:T(8,128)(2,1)S(1)}, bf16[3,64,64]{2,1,0:T(8,128)(2,1)}, u32[]{:S(2)}) copy-start(bf16[3,64,64]{2,1,0:T(8,128)(2,1)} %get-tuple-element.21) | copy-start | bytes 73732
  224.3 23.6 %copy-start.10 = (bf16[3,64,64]{2,1,0:T(8,128)(2,1)S(1)}, bf16[3,64,64]{2,1,0:T(8,128)(2,1)}, u32[]{:S(2)}) copy-start(bf16[3,64,64]{2,1,0:T(8,128)(2,1)} %get-tuple-element.20) | copy-start | bytes 73732
  224.3 24.3 %copy-start.8 = (bf16[3,64,64]{2,1,0:T(8,128)(2,1)S(1)}, bf16[3,64,64]{2,1,0:T(8,128)(2,1)}, u32[]{:S(2)}) copy-start(bf16[3,64,64]{2,1,0:T(8,128)(2,1)} %get-tuple-element.19) | copy-start | bytes 73732
  242.0 26.7 %copy-start.2 = (bf16[24,768,128]{2,1,0:T(8,128)(2,1)}, bf16[24,768,128]{2,1,0:T(8,128)(2,1)S(1)}, u32[]{:S(2)}) copy-start(bf16[24,768,128]{2,1,0:T(8,128)(2,1)S(1)} %fusion.3) | copy-start | bytes 14155780
  242.0 7.6 %collective-permute-start = (bf16[1,768,128]{2,1,0:T(8,128)(2,1)S(1)}, bf16[1,768,128]{2,1,0:T(8,128)(2,1)S(1)}, u32[]{:S(2)}, u32[]{:S(2)}) collective-permute-start(bf16[1,768,128]{2,1,0:T(8,128)(2,1)S(1)} %get-tuple-element.11), channel_id=1, source_target_pairs={{0,1},{1,2},{2,3},{3,4},{4,5},{5,6},{6,7},{7,8},{8,9},{9,10},{10,1... | collective-permute-start | bytes 589832 | tf_op jit(solution)/shard_map/ppermute | solution.py:15
  245.4 9.7 %collective-permute-start.1 = (bf16[1,768,128]{2,1,0:T(8,128)(2,1)S(1)}, bf16[1,768,128]{2,1,0:T(8,128)(2,1)S(1)}, u32[]{:S(2)}, u32[]{:S(2)}) collective-permute-start(bf16[1,768,128]{2,1,0:T(8,128)(2,1)S(1)} %get-tuple-element.12), channel_id=1, source_target_pairs={{1,0},{2,1},{3,2},{4,3},{5,4},{6,5},{7,6},{8,7},{9,8},{10,9},{11,1... | collective-permute-start | bytes 589832 | tf_op jit(solution)/shard_map/ppermute | solution.py:17
  260.0 8.7 %copy-start.3 = (bf16[26,768,128]{2,1,0:T(8,128)(2,1)}, bf16[26,768,128]{2,1,0:T(8,128)(2,1)S(1)}, u32[]{:S(2)}) copy-start(bf16[26,768,128]{2,1,0:T(8,128)(2,1)S(1)} %get-tuple-element.7) | copy-start | bytes 15335428
  260.0 8.7 %copy-start.4 = (bf16[26,768,128]{2,1,0:T(8,128)(2,1)}, bf16[26,768,128]{2,1,0:T(8,128)(2,1)S(1)}, u32[]{:S(2)}) copy-start(bf16[26,768,128]{2,1,0:T(8,128)(2,1)S(1)} %get-tuple-element.8) | copy-start | bytes 15335428
  288.3 24.2 %copy-start.19 = (bf16[3,384,128]{2,1,0:T(8,128)(2,1)S(1)}, bf16[3,384,128]{2,1,0:T(8,128)(2,1)}, u32[]{:S(2)}) copy-start(bf16[3,384,128]{2,1,0:T(8,128)(2,1)} %maximum_dynamic-update-slice_fusion.2) | copy-start | bytes 884740
  306.7 7.6 %collective-permute-start.2 = (bf16[1,768,128]{2,1,0:T(8,128)(2,1)S(1)}, bf16[1,768,128]{2,1,0:T(8,128)(2,1)S(1)}, u32[]{:S(2)}, u32[]{:S(2)}) collective-permute-start(bf16[1,768,128]{2,1,0:T(8,128)(2,1)S(1)} %get-tuple-element.9), channel_id=1, source_target_pairs={{0,1},{1,2},{2,3},{3,4},{4,5},{5,6},{6,7},{7,8},{8,9},{9,10},{10,1... | collective-permute-start | bytes 589832 | tf_op jit(solution)/shard_map/ppermute | solution.py:15
  308.6 9.7 %collective-permute-start.3 = (bf16[1,768,128]{2,1,0:T(8,128)(2,1)S(1)}, bf16[1,768,128]{2,1,0:T(8,128)(2,1)S(1)}, u32[]{:S(2)}, u32[]{:S(2)}) collective-permute-start(bf16[1,768,128]{2,1,0:T(8,128)(2,1)S(1)} %get-tuple-element.10), channel_id=1, source_target_pairs={{1,0},{2,1},{3,2},{4,3},{5,4},{6,5},{7,6},{8,7},{9,8},{10,9},{11,1... | collective-permute-start | bytes 589832 | tf_op jit(solution)/shard_map/ppermute | solution.py:17
  323.2 15.5 %slice-start = ((s8[4718592]{0:T(1024)(128)(4,1)}), s8[4194304]{0:T(1024)(128)(4,1)S(1)}, s32[]{:S(2)}) async-start(s8[4718592]{0:T(1024)(128)(4,1)} %bitcast.103), calls=%async_computation.4 | async-start | bytes 8388608
  338.7 20.2 %copy-start.1 = (f32[128,1536]{1,0:T(8,128)S(1)}, f32[128,1536]{1,0:T(8,128)}, u32[]{:S(2)}) copy-start(f32[128,1536]{1,0:T(8,128)} %param.16) | copy-start | bytes 2359300
  (9 other events, 58.8 us)
Sparse Core Ops, SparseCore 0:
  111.6 52.7 reduce-scatter.1
